TPU v7x, 32 devices: a whole 2x2x4 slice. The times are simulated.
32 devices in a mesh: seq: 4 (over y, core), fsdp: 2 (over x), dp: 4 (over z).
Axes of the slice: x: 2, y: 2, z: 4, core: 2. Of those that a mesh axis runs over, the one named last changes fastest.
Arguments:
- queries: bfloat16 [8, 1024, 4096], P(('fsdp', 'dp'), 'seq'), may hold values from -160 to 160
- hidden: bfloat16 [8, 1024, 8192], P(('fsdp', 'dp'), 'seq'), may hold values from -8 to 8
- key_weight: bfloat16 [8192, 512], P('fsdp'), may hold values from -1 to 1
- doc_lengths: int32 [8, 8], P(('fsdp', 'dp')), may hold values from 1 to 256, 1024 in all within a row
- entropy_cot: bfloat16 [8, 1024, 32], P(('fsdp', 'dp'), 'seq'), may hold values from -600 to 600
Outputs:
- entropy: float32 [8, 1024, 32], P(('fsdp', 'dp'), 'seq')
- grad_queries: bfloat16 [8, 1024, 4096], P(('fsdp', 'dp'), 'seq')
- grad_key_weight: bfloat16 [8192, 512], P('fsdp')
Inputs may be any that keep to these rules, and one draw needn't show every extreme that they name: `doc_lengths`: each sequence's 8 documents are packed in order, their lengths sum to 1024, and the longest is exactly 256.
All inputs are finite; a program needn't handle non-finite values.
Results may differ from a plain program's by a relative error of at most 0.0088.
Values may be sent and summed in bfloat16 or wider, within the bound.
A program may use at most 128 MiB of HBM per device.

v0:
```python
import functools

import jax
import jax.numpy as jnp
from jax import lax
from jax.experimental import pallas as pl
from jax.experimental.pallas import tpu as pltpu
from jax.sharding import PartitionSpec as P


QH = 32
KVH = 4
HD = 128


def from_behind(shard, axis, by):
    length = lax.axis_size(axis)
    pairs = [(i, i + by) for i in range(length) if 0 <= i + by < length]
    return lax.ppermute(shard, axis, pairs)


def document_index(lengths, seq_len):
    ends = jnp.cumsum(lengths)
    position = jnp.arange(seq_len, dtype=jnp.int32)
    return jnp.sum((ends[None, :] <= position[:, None]).astype(jnp.int32), axis=1)


def attend(queries, key_rows, cotangent, doc_index, anchor, doc_len):
    row_count, key_heads, group_size, head_size = queries.shape
    full_len = key_rows.shape[0]
    block_rows = min(512, row_count)
    window = block_rows + doc_len
    factor = head_size ** (-0.5)
    keys_padded = jnp.concatenate(
        [jnp.zeros((doc_len, key_heads, head_size), key_rows.dtype), key_rows], axis=0
    )
    index_padded = jnp.concatenate([jnp.full((doc_len,), -1, jnp.int32), doc_index], axis=0)

    def one_block(step_index, state_now):
        entropy, grad_query, grad_key = state_now
        row_start = (step_index * block_rows).astype(jnp.int32)
        position = anchor + row_start
        weight_block = cotangent.astype(jnp.float32)
        key_block = lax.dynamic_slice_in_dim(keys_padded, position, window, 0)
        key_docs = lax.dynamic_slice_in_dim(index_padded, position, window, 0)
        query_docs = lax.dynamic_slice_in_dim(doc_index, position, block_rows, 0)
        query_pos = position + jnp.arange(block_rows, dtype=jnp.int32)
        key_pos = position - doc_len + jnp.arange(window, dtype=jnp.int32)
        visible = (query_docs[:, None] == key_docs[None, :]) & (
            key_pos[None, :] <= query_pos[:, None]
        )
        scores = (
            jnp.einsum("rkgd,wkd->kgrw", queries, key_block, preferred_element_type=jnp.float32)
            * factor
        )
        scores = jnp.where(visible, scores, -1e30)
        row_max = jnp.max(scores, axis=-1, keepdims=True)
        powers = jnp.exp(scores - row_max)
        denominator = jnp.sum(powers, axis=-1, keepdims=True)
        probability = powers / denominator
        mean_score = jnp.sum(jnp.where(visible, probability * scores, 0.0), axis=-1, keepdims=True)
        block_entropy = (row_max + jnp.log(denominator) - mean_score)[..., 0]
        row_weight = jnp.transpose(weight_block, (1, 2, 0))[..., None]
        slope = jnp.where(visible, row_weight * probability * (mean_score - scores), 0.0).astype(
            jnp.bfloat16
        )
        query_part = (
            jnp.einsum("kgrw,wkd->rkgd", slope, key_block, preferred_element_type=jnp.float32)
            * factor
        )
        key_part = (
            jnp.einsum("kgrw,rkgd->wkd", slope, queries, preferred_element_type=jnp.float32)
            * factor
        )
        entropy = jnp.transpose(block_entropy, (2, 0, 1))
        grad_query = query_part
        previous = lax.dynamic_slice_in_dim(grad_key, position, window, 0)
        grad_key = lax.dynamic_update_slice_in_dim(grad_key, previous + key_part, position, 0)
        return (entropy, grad_query, grad_key)

    initial = (
        jnp.zeros((row_count, key_heads, group_size), jnp.float32),
        jnp.zeros((row_count, key_heads, group_size, head_size), jnp.float32),
        jnp.zeros((full_len + doc_len, key_heads, head_size), jnp.float32),
    )
    entropy, grad_query, grad_key = lax.fori_loop(0, row_count // block_rows, one_block, initial)
    return (entropy, grad_query, grad_key[doc_len:])


def per_head(query_four, key_rows, cot_three, doc_index, anchor, doc_len):
    outcome = [
        attend(
            query_four[:, head_index : head_index + 1],
            key_rows[:, head_index : head_index + 1],
            cot_three[:, head_index : head_index + 1],
            doc_index,
            anchor,
            doc_len,
        )
        for head_index in range(query_four.shape[1])
    ]
    entropy = jnp.concatenate([item_set[0] for item_set in outcome], axis=1)
    grad_query = jnp.concatenate([item_set[1] for item_set in outcome], axis=1)
    grad_key = jnp.concatenate([item_set[2] for item_set in outcome], axis=1)
    return (entropy, grad_query, grad_key)


def after(value, *earlier):
    return lax.optimization_barrier((value, *earlier))[0]


def pair_count(seq_parts):
    return 2 if seq_parts % 2 == 0 else 1


def shift_plane(value, df, dy, dc):
    fsdp, parts = lax.axis_size("fsdp"), lax.axis_size("seq")
    cores = pair_count(parts)
    chips = parts // cores
    pairs = [
        ((y * cores + c) * fsdp + f, (((y + dy) % chips) * cores + (c ^ dc)) * fsdp + (f + df) % fsdp)
        for f in range(fsdp)
        for y in range(chips)
        for c in range(cores)
    ]
    return lax.ppermute(value, ("seq", "fsdp"), pairs)


MESH = pl.DeviceIdType.MESH


def tail_kernel(fsdp, chips, cores, depth, share, norm, *refs):
    count = fsdp * chips * cores
    key_ref, token_refs, out_ref = refs[0], refs[1 : 1 + count], refs[1 + count]
    held, acc, parts, landed, final, send, recv, local = refs[2 + count :]
    slab = depth * share
    f, s, z = lax.axis_index("fsdp"), lax.axis_index("seq"), lax.axis_index("dp")
    y, c = lax.div(s, cores), lax.rem(s, cores)

    def seq_at(dy, dc):
        other = c if dc == 0 else 1 - c
        return {"seq": lax.rem(y + dy + chips, chips) * cores + other}

    def fsdp_at(df):
        return {"fsdp": lax.rem(f + df, fsdp)}

    partners = [fsdp_at(df) for df in range(1, fsdp)]
    partners += [seq_at(dy, 0) for dy in range(1, chips)]
    partners += [seq_at(0, 1)] * (cores - 1)
    partners += [{"dp": lax.rem(z + dz, depth)} for dz in range(1, depth)]
    barrier = pltpu.get_barrier_semaphore()
    for device in partners:
        pl.semaphore_signal(barrier, inc=1, device_id=device, device_id_type=MESH)
    pl.semaphore_wait(barrier, len(partners))

    numbers = {}

    def remote(name, src, dst, device):
        slot = numbers.setdefault(name, len(numbers))
        return pltpu.make_async_remote_copy(
            src_ref=src,
            dst_ref=dst,
            send_sem=send.at[slot],
            recv_sem=recv.at[slot],
            device_id=device,
            device_id_type=MESH,
        )

    def place(df, dy, dc):
        return (df * chips + dy) * cores + dc

    def plane_copy(df, dy, dc):
        if dc:
            source, device = (df, dy, 0), seq_at(0, 1)
        elif dy:
            source, device = (df, 0, 0), seq_at(dy, 0)
        else:
            source, device = (0, 0, 0), fsdp_at(df)
        src = key_ref if source == (0, 0, 0) else held.at[place(*source)]
        return remote(("key", df, dy, dc), src, held.at[place(df, dy, dc)], device)

    def follow(df, dy, dc):
        if dc == 0:
            if dy == 0:
                for step in range(1, chips):
                    plane_copy(df, step, 0).start()
            if cores == 2:
                plane_copy(df, dy, 1).start()

    tile = min(256, slab)

    def accumulate(df, dy, dc):
        number = place(df, dy, dc)
        token_ref = token_refs[number]
        rows_ref = key_ref if number == 0 else held.at[number]

        @pl.loop(0, slab // tile)
        def _(step):
            at = pl.ds(pl.multiple_of(step * tile, tile), tile)
            value = lax.dot_general(
                token_ref[:, at], rows_ref[...], (((0,), (0,)), ((), ())),
                preferred_element_type=jnp.float32,
            )
            if number == 0:
                acc[at, :] = value
            else:
                acc[at, :] += value

    for df in range(1, fsdp):
        plane_copy(df, 0, 0).start()
    follow(0, 0, 0)
    accumulate(0, 0, 0)
    near = [(0, dy, 0) for dy in range(1, chips)] + [(df, 0, 0) for df in range(1, fsdp)]
    far = [(df, dy, 0) for df in range(1, fsdp) for dy in range(1, chips)]
    last = [(df, dy, 1) for df in range(fsdp) for dy in range(chips) if cores == 2]
    for group in (near, last[:1], far, last[1:]):
        for item in group:
            plane_copy(*item).wait_recv()
            follow(*item)
        for item in group:
            accumulate(*item)

    def part_copy(dz):
        return remote(
            ("part", dz), parts.at[dz - 1], landed.at[dz - 1], {"dp": lax.rem(z + dz, depth)}
        )

    for dz in range(1, depth):
        row = pl.multiple_of(lax.rem(z + dz, depth) * share, share)
        parts[dz - 1] = acc[pl.ds(row, share), :].astype(jnp.bfloat16)
        part_copy(dz).start()
    total = acc[pl.ds(pl.multiple_of(z * share, share), share), :]
    for dz in range(1, depth):
        part_copy(dz).wait_recv()
        total = total + landed[dz - 1].astype(jnp.float32)
    final[...] = (total * norm).astype(jnp.bfloat16)

    def rows(dy, dc, zz):
        chip = lax.rem(y - dy + chips, chips)
        core = c if dc == 0 else 1 - c
        row = ((chip * cores + core) * depth + zz) * share
        return out_ref.at[pl.ds(pl.multiple_of(row, share), share)]

    def event_depth(event):
        way, step = event
        return z if way == 0 else z - way * (step + 1)

    def event_live(event):
        where = event_depth(event)
        return (where >= 0) & (where < depth)

    def block_of(event):
        return final if event[0] == 0 else rows(0, 0, event_depth(event))

    def depth_copy(event):
        way, step = event
        where = z - way * step
        src = final if step == 0 else rows(0, 0, where)
        return remote(("z", event), src, rows(0, 0, where), {"dp": z + way})

    def depth_live(event):
        way, step = event
        where = z - way * step
        return (where >= 0) & (where < depth) & (z + way >= 0) & (z + way < depth)

    def row_copy(event, dy, dc):
        where = event_depth(event)
        if dc:
            return remote(
                ("c", event, dy), rows(dy, 0, where) if dy else block_of(event),
                rows(dy, 0, where), seq_at(0, 1),
            )
        return remote(("y", event, dy), block_of(event), rows(0, 0, where), seq_at(dy, 0))

    own = (0, 0)
    events = [own] + [(way, step) for step in range(depth - 1) for way in (1, -1)]
    own_copy = pltpu.make_async_copy(final, rows(0, 0, z), local)
    own_copy.start()

    def when(event, live, action):
        if event == own:
            action()
        else:
            pl.when(live(event))(action)

    def spread(event):
        for dy in range(1, chips):
            row_copy(event, dy, 0).start()
        if cores == 2:
            row_copy(event, 0, 1).start()

    def arrive(event):
        if event != own:
            depth_copy(event).wait_recv()
        spread(event)

    def relay(event):
        for dy in range(1, chips):
            row_copy(event, dy, 0).wait_recv()
            if cores == 2:
                row_copy(event, dy, 1).start()

    def close(event):
        for dy in range(1, chips):
            row_copy(event, dy, 0).wait_send()
        if cores == 2:
            for dy in range(chips):
                row_copy(event, dy, 1).wait()

    for way in (1, -1):
        if depth > 1:
            when((way, 0), depth_live, lambda way=way: depth_copy((way, 0)).start())
    before = None
    for event in events:
        when(event, event_live, functools.partial(arrive, event))
        if event != own and event[1] + 1 < depth - 1:
            after_it = (event[0], event[1] + 1)
            when(after_it, depth_live, lambda after_it=after_it: depth_copy(after_it).start())
        if before is not None:
            when(before, event_live, functools.partial(relay, before))
        before = event
    when(before, event_live, functools.partial(relay, before))
    for event in events:
        when(event, event_live, functools.partial(close, event))
        if event != own:
            when(event, depth_live, lambda event=event: depth_copy(event).wait_send())
    own_copy.wait()
    for df in range(fsdp):
        for dy in range(chips):
            for dc in range(cores):
                if (df, dy, dc) != (0, 0, 0):
                    plane_copy(df, dy, dc).wait_send()
    for dz in range(1, depth):
        part_copy(dz).wait_send()


def tail(key_grad, token_blocks, norm):
    fsdp, parts, depth = lax.axis_size("fsdp"), lax.axis_size("seq"), lax.axis_size("dp")
    cores = pair_count(parts)
    chips = parts // cores
    count = len(token_blocks)
    rows, slab = token_blocks[0].shape
    width = key_grad.shape[1]
    share = slab // depth
    copies = count - 1 + depth - 1 + 2 * (depth - 1) + (2 * depth - 1) * (chips - 1 + chips)
    return pl.pallas_call(
        functools.partial(tail_kernel, fsdp, chips, cores, depth, share, norm),
        out_shape=jax.ShapeDtypeStruct((slab * parts, width), jnp.bfloat16),
        in_specs=[pl.BlockSpec(memory_space=pltpu.VMEM)] * (1 + count),
        out_specs=pl.BlockSpec(memory_space=pl.ANY),
        scratch_shapes=[
            pltpu.VMEM((count, rows, width), jnp.bfloat16),
            pltpu.VMEM((slab, width), jnp.float32),
            pltpu.VMEM((max(depth - 1, 1), share, width), jnp.bfloat16),
            pltpu.VMEM((max(depth - 1, 1), share, width), jnp.bfloat16),
            pltpu.VMEM((share, width), jnp.bfloat16),
            pltpu.SemaphoreType.DMA((copies,)),
            pltpu.SemaphoreType.DMA((copies,)),
            pltpu.SemaphoreType.DMA(()),
        ],
        compiler_params=pltpu.CompilerParams(collective_id=0, has_side_effects=True),
        name="tail",
    )(key_grad, *token_blocks)


def project_kernel(fsdp, chips, cores, chunks, token_hbm, weight_hbm, ext_ref, *scratch):
    tokens, weight, gathered, acc, key_out, before, send, recv, local = scratch
    parts = chips * cores
    rows = tokens.shape[0]
    shard = weight.shape[0]
    slab = shard // parts
    chunk = slab // chunks
    f, s = lax.axis_index("fsdp"), lax.axis_index("seq")
    y, c = lax.div(s, cores), lax.rem(s, cores)

    def seq_of(dy, dc):
        other = c if dc == 0 else 1 - c
        return lax.rem(y + dy + chips, chips) * cores + other

    partners = [{"fsdp": lax.rem(f + df, fsdp)} for df in range(1, fsdp)]
    partners += [{"seq": seq_of(dy, 0)} for dy in range(1, chips)]
    partners += [{"seq": seq_of(0, 1)}] * (cores - 1)
    if parts > 1:
        partners += [{"seq": lax.rem(s + 1, parts)}, {"seq": lax.rem(s + parts - 1, parts)}]
    barrier = pltpu.get_barrier_semaphore()
    for device in partners:
        pl.semaphore_signal(barrier, inc=1, device_id=device, device_id_type=MESH)
    token_copy = pltpu.make_async_copy(token_hbm, tokens, local.at[0])
    weight_copy = pltpu.make_async_copy(weight_hbm, weight, local.at[1])
    token_copy.start()
    weight_copy.start()
    pl.semaphore_wait(barrier, len(partners))

    numbers = {}

    def remote(name, src, dst, device):
        slot = numbers.setdefault(name, len(numbers))
        return pltpu.make_async_remote_copy(
            src_ref=src,
            dst_ref=dst,
            send_sem=send.at[slot],
            recv_sem=recv.at[slot],
            device_id=device,
            device_id_type=MESH,
        )

    def span(owner, k, count=1):
        return pl.ds(pl.multiple_of(owner * slab + k * chunk, chunk), count * chunk)

    def first(df, k):
        at = span(s, k)
        return remote(
            (df, k), weight_hbm.at[at], gathered.at[df - 1, at], {"fsdp": lax.rem(f + df, fsdp)}
        )

    def along(df, k, dy):
        at = span(s, k)
        piece = gathered.at[df - 1, at]
        return remote((df, k, "y", dy), piece, piece, {"seq": seq_of(dy, 0)})

    def across(df, k, dy):
        at = span(seq_of(-dy, 0), k)
        piece = gathered.at[df - 1, at]
        return remote((df, k, "c", dy), piece, piece, {"seq": seq_of(0, 1)})

    shards_in = range(1, fsdp)
    for k in range(chunks):
        for df in shards_in:
            first(df, k).start()
    token_copy.wait()
    weight_copy.wait()
    step = shard // chunks
    group = 2 if chunks % 2 == 0 else 1

    def own_part(k):
        at = pl.ds(pl.multiple_of(f * shard + k * step, step), step)
        value = jnp.dot(
            tokens[:, at], weight[k * step : (k + 1) * step, :],
            preferred_element_type=jnp.float32,
        )
        if k == 0:
            acc[...] = value
        else:
            acc[...] += value

    def landed(k):
        for df in shards_in:
            first(df, k).wait_recv()
            for dy in range(1, chips):
                along(df, k, dy).start()
            if cores == 2:
                across(df, k, 0).start()

    def passed(k):
        for df in shards_in:
            for dy in range(1, chips):
                along(df, k, dy).wait_recv()
                if cores == 2:
                    across(df, k, dy).start()

    def used(k):
        if cores == 2:
            for df in shards_in:
                for dy in range(chips):
                    across(df, k, dy).wait_recv()
        if (k + 1) % group == 0:
            begin = k + 1 - group
            for df in shards_in:
                owner = lax.rem(f - df + fsdp, fsdp) * shard
                value = None
                for dy in range(chips):
                    for dc in range(cores):
                        holder = seq_of(-dy, dc)
                        columns = owner + holder * slab + begin * chunk
                        at = pl.ds(pl.multiple_of(columns, group * chunk), group * chunk)
                        term = jnp.dot(
                            tokens[:, at], gathered[df - 1, span(holder, begin, group), :],
                            preferred_element_type=jnp.float32,
                        )
                        value = term if value is None else value + term
                acc[...] += value

    for k in range(chunks + 2):
        if k < chunks:
            own_part(k)
            landed(k)
        if 1 <= k <= chunks:
            passed(k - 1)
        if k >= 2:
            used(k - 2)

    key_out[...] = acc[...].astype(key_out.dtype)
    halo = remote("halo", key_out, before, {"seq": lax.rem(s + 1, parts)})

    @pl.when(s + 1 < parts)
    def _():
        halo.start()

    ext_ref[rows:, :] = key_out[...]

    @pl.when(s == 0)
    def _():
        ext_ref[:rows, :] = jnp.zeros_like(key_out)

    @pl.when(s > 0)
    def _():
        halo.wait_recv()
        ext_ref[:rows, :] = before[...]

    @pl.when(s + 1 < parts)
    def _():
        halo.wait_send()

    for k in range(chunks):
        for df in shards_in:
            first(df, k).wait_send()
            for dy in range(1, chips):
                along(df, k, dy).wait_send()
            if cores == 2:
                for dy in range(chips):
                    across(df, k, dy).wait_send()


def project(tokens, key_weight):
    fsdp, parts = lax.axis_size("fsdp"), lax.axis_size("seq")
    cores = pair_count(parts)
    chips = parts // cores
    rows = tokens.shape[0]
    shard, width = key_weight.shape
    chunks = max(1, min(8, shard // parts // 128))
    copies = (fsdp - 1) * chunks * (1 + chips - 1 + chips) + 1
    return pl.pallas_call(
        functools.partial(project_kernel, fsdp, chips, cores, chunks),
        out_shape=jax.ShapeDtypeStruct((2 * rows, width), jnp.bfloat16),
        in_specs=[pl.BlockSpec(memory_space=pl.ANY)] * 2,
        out_specs=pl.BlockSpec(memory_space=pltpu.VMEM),
        scratch_shapes=[
            pltpu.VMEM(tokens.shape, tokens.dtype),
            pltpu.VMEM(key_weight.shape, key_weight.dtype),
            pltpu.VMEM((max(fsdp - 1, 1), shard, width), key_weight.dtype),
            pltpu.VMEM((rows, width), jnp.float32),
            pltpu.VMEM((rows, width), jnp.bfloat16),
            pltpu.VMEM((rows, width), jnp.bfloat16),
            pltpu.SemaphoreType.DMA((copies,)),
            pltpu.SemaphoreType.DMA((copies,)),
            pltpu.SemaphoreType.DMA((2,)),
        ],
        compiler_params=pltpu.CompilerParams(collective_id=1, has_side_effects=True),
        name="project",
    )(tokens, key_weight)


def shards(queries, hidden, key_weight, doc_lengths, entropy_cot):
    tokens = hidden[0]
    local_rows, width = tokens.shape
    seq_parts = lax.axis_size("seq")
    fsdp_parts = lax.axis_size("fsdp")
    dp_parts = lax.axis_size("dp")
    cores = pair_count(seq_parts)
    chips = seq_parts // cores
    f_pos, s_pos = lax.axis_index("fsdp"), lax.axis_index("seq")
    y_pos, c_pos = s_pos // cores, s_pos % cores
    shard_rows = width // fsdp_parts
    slab = shard_rows // seq_parts
    seq_len = local_rows * seq_parts
    group_size = QH // KVH
    doc_index = document_index(doc_lengths[0], seq_len)

    def seq_at(dy, dc):
        return ((y_pos + dy) % chips) * cores + (c_pos ^ dc)

    def column_slab(f, s, start, count):
        return lax.dynamic_slice_in_dim(tokens, f * shard_rows + s * slab + start, count, 1)

    ext_keys = project(tokens, key_weight)

    plane = [
        (df, dy, dc) for df in range(fsdp_parts) for dy in range(chips) for dc in range(cores)
    ]
    token_blocks = []
    for df, dy, dc in plane:
        block = column_slab((f_pos + df) % fsdp_parts, seq_at(dy, dc), 0, slab)
        if (df, dy, dc) != (0, 0, 0):
            block = after(block, ext_keys)
            block = shift_plane(block, df, dy, dc)
        token_blocks.append(block)

    query_local = queries[0]
    cot_local = entropy_cot[0]
    start = s_pos * local_rows
    prev_index = lax.dynamic_slice_in_dim(
        doc_index, jnp.maximum(start - local_rows, 0), local_rows, 0
    )
    prev_index = jnp.where(s_pos > 0, prev_index, -1)
    own_index = lax.dynamic_slice_in_dim(doc_index, start, local_rows, 0)
    ext_index = jnp.concatenate([prev_index, own_index], axis=0)
    ext_keys = ext_keys.reshape(2 * local_rows, KVH, HD)
    entropy_heads, grad_heads, key_heads_ext = per_head(
        query_local.reshape(local_rows, KVH, group_size, HD),
        ext_keys,
        cot_local.reshape(local_rows, KVH, group_size),
        ext_index,
        local_rows,
        local_rows,
    )
    entropy_local = entropy_heads.reshape(local_rows, QH)
    grad_local = grad_heads.reshape(local_rows, QH * HD)
    key_ext = key_heads_ext.reshape(2 * local_rows, KVH * HD)
    returned = from_behind(key_ext[:local_rows], "seq", -1)
    key_grad = (key_ext[local_rows:] + returned).astype(jnp.bfloat16)

    token_blocks = [after(block, key_grad) for block in token_blocks]

    norm_factor = (seq_len * fsdp_parts * dp_parts) ** (-0.5)
    grad_local = grad_local.astype(jnp.bfloat16)
    key_grad, entropy_local, grad_local = lax.optimization_barrier(
        (key_grad, entropy_local, grad_local)
    )
    weight_grad = tail(key_grad, token_blocks, norm_factor)
    return (
        entropy_local.reshape(1, local_rows, QH),
        grad_local.reshape(1, local_rows, QH * HD),
        weight_grad,
    )


def solution(mesh):
    return jax.shard_map(
        shards,
        mesh=mesh,
        in_specs=(
            P(("fsdp", "dp"), "seq", None),
            P(("fsdp", "dp"), "seq", None),
            P("fsdp", None),
            P(("fsdp", "dp"), None),
            P(("fsdp", "dp"), "seq", None),
        ),
        out_specs=(P(("fsdp", "dp"), "seq", None), P(("fsdp", "dp"), "seq", None), P("fsdp", None)),
        check_vma=False,
    )
```

profile of v0, /device:TPU:0, one launch (start us, length us, event | category | flops | bytes accessed | tf_op | source)
XLA Modules:
  0.0 224.9 jit_solution(1882383087669205651)
XLA Ops:
  0.6 3.3 %copy.60 = bf16[1,256,4096]{1,2,0:T(8,128)(2,1)S(1)} copy(bf16[1,256,4096]{2,1,0:T(8,128)(2,1)} %param.5) | data formatting | bytes 4194304 | tf_op args[0]
  3.9 35.4 %project.1 = bf16[512,512]{1,0:T(8,128)(2,1)} custom-call(bf16[256,8192]{1,0:T(8,128)(2,1)} %bitcast.324, bf16[4096,512]{1,0:T(8,128)(2,1)} %weight_hbm.1), custom_call_target="tpu_custom_call" | custom-call | tf_op jit(solution)/shard_map/project/pallas_call | solution.py:532
  39.3 1.2 reshape.347
  40.5 1.4 fusion.106
  42.2 2.7 %fusion.104 = f32[512,256,8]{1,0,2:T(8,128)} fusion(bf16[256,4,8,128]{0,3,2,1:T(8,128)(2,1)S(1)} %bitcast.326, bf16[512,1,128]{2,1,0:T(2,128)(2,1)S(1)} %get-tuple-element.174), kind=kOutput, calls=%fused_computation.88 | convolution fusion | flops 268435456 | bytes 4980736 | tf_op jit(solution)/shard_map/while/body/eval_jaxpr/rkgd,wkd->kgrw/dot_general | solution.py:53
  44.9 2.7 %fusion.103 = f32[512,256,8]{1,0,2:T(8,128)} fusion(bf16[256,4,8,128]{0,3,2,1:T(8,128)(2,1)S(1)} %bitcast.327, bf16[512,1,128]{2,1,0:T(2,128)(2,1)S(1)} %get-tuple-element.171), kind=kOutput, calls=%fused_computation.87 | convolution fusion | flops 268435456 | bytes 4980736 | tf_op jit(solution)/shard_map/while/body/eval_jaxpr/rkgd,wkd->kgrw/dot_general | solution.py:53
  50.2 1.4 copy-done
  51.6 1.8 copy-done.2
  53.5 3.6 %select_reduce_fusion.3 = (f32[8,256]{1,0:T(8,128)S(1)}, f32[8,256]{1,0:T(8,128)S(1)}, f32[8,256]{1,0:T(8,128)S(1)}, f32[8,256]{1,0:T(8,128)S(1)}, f32[512,256,8]{1,0,2:T(8,128)S(1)}) fusion(f32[512,256,8]{1,0,2:T(8,128)S(1)} %get-tuple-element.182, f32[8,256]{1,0:T(8,128)S(1)} %fusion.1, f32[8,256]{1,0:T(8,128)S(1)} %get-tuple-element.181, ...), kind=kOutput, calls=%fused_computation.14 | convolution fusion | flops 285204480 | bytes 17743872 | tf_op jit(solution)/shard_map/while/body/eval_jaxpr/rkgd,wkd->kgrw/dot_general | solution.py:53
  57.1 2.9 %fusion.3 = (f32[8,256]{1,0:T(8,128)S(1)}, f32[8,256]{1,0:T(8,128)S(1)}, f32[8,256]{1,0:T(8,128)S(1)}) fusion(f32[512,256,8]{1,0,2:T(8,128)S(1)} %get-tuple-element.183, f32[8,256]{1,0:T(8,128)S(1)} %get-tuple-element.142, pred[256,512]{0,1:T(8,128)(4,1)S(1)} %fusion.100, f32[8,256]{1,0:T(8,128)S(1)} %get-tuple-element.143, f32[512,256,8]{1,0,2:T(8,128)S(1)} %copy-done, ...), kind=kLoop, calls=%fused_computation.19 | loop fusion | flops 12576768 | bytes 12763136 | tf_op jit(solution)/shard_map/while/body/eval_jaxpr/reduce_sum | solution.py:59
  60.0 4.3 %select_reduce_fusion.2 = (f32[8,256]{1,0:T(8,128)S(1)}, f32[8,256]{1,0:T(8,128)S(1)}, f32[8,256]{1,0:T(8,128)S(1)}) fusion(f32[512,256,8]{1,0,2:T(8,128)S(1)} %get-tuple-element.183, f32[8,256]{1,0:T(8,128)S(1)} %get-tuple-element.148, f32[8,256]{1,0:T(8,128)S(1)} %get-tuple-element.142, pred[256,512]{0,1:T(8,128)(4,1)S(1)} %fusion.100, ...), kind=kLoop, calls=%fused_computation.11 | loop fusion | flops 22013952 | bytes 12787712 | tf_op jit(solution)/shard_map/while/body/eval_jaxpr/reduce_sum | solution.py:61
  64.5 1.8 fusion.79
  66.3 1.8 fusion.85
  68.2 1.8 fusion.91
  70.0 1.8 fusion.97
  73.0 1.5 collective-permute-start
  74.7 4.4 %dynamic-slice_bitcast_fusion = (bf16[256,1024]{1,0:T(8,128)(2,1)}, bf16[256,1024]{1,0:T(8,128)(2,1)}, bf16[256,1024]{1,0:T(8,128)(2,1)}, bf16[256,1024]{1,0:T(8...) fusion(bf16[1,256,8192]{2,1,0:T(8,128)(2,1)} %param.6, ...), kind=kLoop, calls=%fused_computation.74 | loop fusion | bytes 8388640 | tf_op jit(solution)/shard_map/dynamic_slice | solution.py:573
  79.1 4.0 %collective-permute-start.1 = (bf16[256,1024]{1,0:T(8,128)(2,1)}, bf16[256,1024]{1,0:T(8,128)(2,1)S(1)}, u32[]{:S(2)}, u32[]{:S(2)}) collective-permute-start(bf16[256,1024]{1,0:T(8,128)(2,1)} %get-tuple-element.107), channel_id=1, source_target_pairs={{0,8},{8,0},{16,24},{24,16},{4,12},{12,4},{20,28},{28,20},{1,9},{9... | collective-permute-start | bytes 1572872 | tf_op jit(solution)/shard_map/ppermute | solution.py:126
  83.1 2.9 %collective-permute-start.2 = (bf16[256,1024]{1,0:T(8,128)(2,1)}, bf16[256,1024]{1,0:T(8,128)(2,1)S(1)}, u32[]{:S(2)}, u32[]{:S(2)}) collective-permute-start(bf16[256,1024]{1,0:T(8,128)(2,1)} %get-tuple-element.109), channel_id=1, source_target_pairs={{0,16},{8,24},{16,0},{24,8},{4,20},{12,28},{20,4},{28,12},{1,17},{... | collective-permute-start | bytes 1572872 | tf_op jit(solution)/shard_map/ppermute | solution.py:126
  86.0 1.5 collective-permute-start.4
  88.2 2.6 %fusion.61 = bf16[256,1,8,128]{0,3,2,1:T(8,128)(2,1)} fusion(bf16[512,1,128]{2,1,0:T(2,128)(2,1)S(1)} %get-tuple-element.174, f32[512,256,8]{1,0,2:T(8,128)S(1)} %copy-done.3, f32[8,256]{1,0:T(8,128)S(1)} %copy-done.32, f32[8,256]{1,0:T(8,128)S(1)} %copy-done.23, f32[8,256]{1,0:T(8,128)S(1)} %copy-done.21, f32[8,256]{1,0:T(8,128)S(1)} %copy-done.41, ...), kind=kOutput, calls=%fused_computation.56 | convolution fusion | flops 278396928 | bytes 5013504 | tf_op jit(solution)/shard_map/while/body/eval_jaxpr/kgrw,wkd->rkgd/dot_general | solution.py:68
  90.8 2.6 %fusion.58 = bf16[256,1,8,128]{0,3,2,1:T(8,128)(2,1)} fusion(bf16[512,1,128]{2,1,0:T(2,128)(2,1)S(1)} %get-tuple-element.171, f32[512,256,8]{1,0,2:T(8,128)S(1)} %copy-done.1, f32[8,256]{1,0:T(8,128)S(1)} %copy-done.30, f32[8,256]{1,0:T(8,128)S(1)} %copy-done.19, f32[8,256]{1,0:T(8,128)S(1)} %copy-done.17, f32[8,256]{1,0:T(8,128)S(1)} %copy-done.39, ...), kind=kOutput, calls=%fused_computation.55 | convolution fusion | flops 278396928 | bytes 5013504 | tf_op jit(solution)/shard_map/while/body/eval_jaxpr/kgrw,wkd->rkgd/dot_general | solution.py:68
  93.4 2.6 %fusion.55 = bf16[256,1,8,128]{0,3,2,1:T(8,128)(2,1)} fusion(bf16[512,1,128]{2,1,0:T(2,128)(2,1)S(1)} %copy-done.13, f32[512,256,8]{1,0,2:T(8,128)S(1)} %copy-done.7, f32[8,256]{1,0:T(8,128)S(1)} %copy-done.28, f32[8,256]{1,0:T(8,128)S(1)} %copy-done.15, f32[8,256]{1,0:T(8,128)S(1)} %get-tuple-element.142, f32[8,256]{1,0:T(8,128)S(1)} %copy-done.37, ...), kind=kOutput, calls=%fused_computation.54 | convolution fusion | flops 278396928 | bytes 5013504 | tf_op jit(solution)/shard_map/while/body/eval_jaxpr/kgrw,wkd->rkgd/dot_general | solution.py:68
  96.0 2.6 %fusion.52 = bf16[256,1,8,128]{0,3,2,1:T(8,128)(2,1)} fusion(bf16[512,1,128]{2,1,0:T(2,128)(2,1)S(1)} %get-tuple-element.173, f32[512,256,8]{1,0,2:T(8,128)S(1)} %copy-done.5, f32[8,256]{1,0:T(8,128)S(1)} %copy-done.43, f32[8,256]{1,0:T(8,128)S(1)} %copy-done.25, f32[8,256]{1,0:T(8,128)S(1)} %get-tuple-element.181, f32[8,256]{1,0:T(8,128)S(1)} %copy-done.35, ...), kind=kOutput, calls=%fused_computation.53 | convolution fusion | flops 278396928 | bytes 5013504 | tf_op jit(solution)/shard_map/while/body/eval_jaxpr/kgrw,wkd->rkgd/dot_general | solution.py:68
  99.0 2.9 %collective-permute-start.6 = (bf16[256,1024]{1,0:T(8,128)(2,1)}, bf16[256,1024]{1,0:T(8,128)(2,1)}, u32[]{:S(2)}, u32[]{:S(2)}) collective-permute-start(bf16[256,1024]{1,0:T(8,128)(2,1)} %get-tuple-element.127), channel_id=1, source_target_pairs={{0,20},{8,28},{16,4},{24,12},{4,16},{12,24},{20,0},{28,8},{1,21},{... | collective-permute-start | bytes 1572872 | tf_op jit(solution)/shard_map/ppermute | solution.py:126
  103.3 1.8 pad_maximum_fusion
  106.0 2.8 %copy.86 = bf16[256,4096]{1,0:T(8,128)(2,1)} copy(bf16[256,4096]{0,1:T(8,128)(2,1)S(1)} %bitcast.325) | data formatting | bytes 4194304 | tf_op jit(solution)/shard_map/optimization_barrier | solution.py:616
  109.7 3.6 %collective-permute-done.5.refs_6_ = bf16[256,1024]{1,0:T(8,128)(2,1)S(1)} collective-permute-done((bf16[256,1024]{1,0:T(8,128)(2,1)}, bf16[256,1024]{1,0:T(8,128)(2,1)S(1)}, u32[]{:S(2)}, u32[]{:S(2)}) %collective-permute-start.5) | collective-permute-done | bytes 524320 | tf_op jit(solution)/shard_map/ppermute | solution.py:126
  113.4 12.8 %collective-permute-done.6.refs_7_ = bf16[256,1024]{1,0:T(8,128)(2,1)} collective-permute-done((bf16[256,1024]{1,0:T(8,128)(2,1)}, bf16[256,1024]{1,0:T(8,128)(2,1)}, u32[]{:S(2)}, u32[]{:S(2)}) %collective-permute-start.6) | collective-permute-done | bytes 524320 | tf_op jit(solution)/shard_map/ppermute | solution.py:126
  126.2 10.0 %collective-permute-done.7.refs_8_ = bf16[256,1024]{1,0:T(8,128)(2,1)} collective-permute-done((bf16[256,1024]{1,0:T(8,128)(2,1)}, bf16[256,1024]{1,0:T(8,128)(2,1)}, u32[]{:S(2)}, u32[]{:S(2)}) %collective-permute-start.7) | collective-permute-done | bytes 524320 | tf_op jit(solution)/shard_map/ppermute | solution.py:126
  136.2 84.3 %tail.1 = bf16[4096,512]{1,0:T(8,128)(2,1)} custom-call(bf16[256,512]{1,0:T(8,128)(2,1)} %add_convert_fusion.refs_0_, bf16[256,1024]{1,0:T(8,128)(2,1)} %get-tuple-element.106.refs_1_, bf16[256,1024]{1,0:T(8,128)(2,1)} %copy-done.8, bf16[256,1024]{1,0:T(8,128)(2,1)} %copy-done.9, bf16[256,1024]{1,0:T(8,128)(2,1)} %collective-permute-done.3.refs_4_, ...), custom_call_target="tpu_custom_call" | custom-call | tf_op jit(solution)/shard_map/tail/pallas_call | solution.py:346
  220.5 4.5 %copy.134 = bf16[4096,512]{1,0:T(8,128)(2,1)} copy(bf16[4096,512]{1,0:T(8,128)(2,1)} %tail.1) | data formatting | bytes 8388608
  (114 shorter events, 8.2 us)
Async XLA Ops:
  3.9 38.0 %copy-start.44 = (s32[1,8]{1,0:T(1,128)S(1)}, s32[1,8]{1,0:T(1,128)}, u32[]{:S(2)}) copy-start(s32[1,8]{1,0:T(1,128)} %param.8) | copy-start | bytes 100
  42.2 5.4 %copy-start.33 = (bf16[1,256,32]{1,2,0:T(8,128)(2,1)S(1)}, bf16[1,256,32]{1,2,0:T(8,128)(2,1)}, u32[]{:S(2)}) copy-start(bf16[1,256,32]{1,2,0:T(8,128)(2,1)} %param.9) | copy-start | bytes 49156
  48.5 3.2 %copy-start = (f32[512,256,8]{1,0,2:T(8,128)S(1)}, f32[512,256,8]{1,0,2:T(8,128)}, u32[]{:S(2)}) copy-start(f32[512,256,8]{1,0,2:T(8,128)} %fusion.103) | copy-start | bytes 12582916
  48.5 5.0 %copy-start.2 = (f32[512,256,8]{1,0,2:T(8,128)S(1)}, f32[512,256,8]{1,0,2:T(8,128)}, u32[]{:S(2)}) copy-start(f32[512,256,8]{1,0,2:T(8,128)} %fusion.104) | copy-start | bytes 12582916
  48.5 5.0 %copy-start.13 = (bf16[512,1,128]{2,1,0:T(2,128)(2,1)S(1)}, bf16[512,1,128]{2,1,0:T(2,128)(2,1)}, u32[]{:S(2)}) copy-start(bf16[512,1,128]{2,1,0:T(2,128)(2,1)} %get-tuple-element.172) | copy-start | bytes 393220
  49.3 20.7 %copy-start.4 = (f32[512,256,8]{1,0,2:T(8,128)}, f32[512,256,8]{1,0,2:T(8,128)S(1)}, u32[]{:S(2)}) copy-start(f32[512,256,8]{1,0,2:T(8,128)S(1)} %get-tuple-element.182) | copy-start | bytes 12582916
  50.2 19.8 %copy-start.24 = (f32[8,256]{1,0:T(8,128)}, f32[8,256]{1,0:T(8,128)S(1)}, u32[]{:S(2)}) copy-start(f32[8,256]{1,0:T(8,128)S(1)} %fusion.1) | copy-start | bytes 24580
  57.1 7.3 %copy-start.20 = (f32[8,256]{1,0:T(8,128)}, f32[8,256]{1,0:T(8,128)S(1)}, u32[]{:S(2)}) copy-start(f32[8,256]{1,0:T(8,128)S(1)} %get-tuple-element.144) | copy-start | bytes 24580
  57.1 9.2 %copy-start.16 = (f32[8,256]{1,0:T(8,128)}, f32[8,256]{1,0:T(8,128)S(1)}, u32[]{:S(2)}) copy-start(f32[8,256]{1,0:T(8,128)S(1)} %get-tuple-element.143) | copy-start | bytes 24580
  57.1 11.0 %copy-start.6 = (f32[512,256,8]{1,0,2:T(8,128)}, f32[512,256,8]{1,0,2:T(8,128)S(1)}, u32[]{:S(2)}) copy-start(f32[512,256,8]{1,0,2:T(8,128)S(1)} %get-tuple-element.183) | copy-start | bytes 12582916
  57.1 12.9 %copy-start.42 = (f32[8,256]{1,0:T(8,128)}, f32[8,256]{1,0:T(8,128)S(1)}, u32[]{:S(2)}) copy-start(f32[8,256]{1,0:T(8,128)S(1)} %get-tuple-element.141) | copy-start | bytes 24580
  60.0 4.4 %copy-start.22 = (f32[8,256]{1,0:T(8,128)}, f32[8,256]{1,0:T(8,128)S(1)}, u32[]{:S(2)}) copy-start(f32[8,256]{1,0:T(8,128)S(1)} %get-tuple-element.160) | copy-start | bytes 24580
  60.0 6.3 %copy-start.18 = (f32[8,256]{1,0:T(8,128)}, f32[8,256]{1,0:T(8,128)S(1)}, u32[]{:S(2)}) copy-start(f32[8,256]{1,0:T(8,128)S(1)} %get-tuple-element.149) | copy-start | bytes 24580
  60.0 8.1 %copy-start.14 = (f32[8,256]{1,0:T(8,128)}, f32[8,256]{1,0:T(8,128)S(1)}, u32[]{:S(2)}) copy-start(f32[8,256]{1,0:T(8,128)S(1)} %get-tuple-element.148) | copy-start | bytes 24580
  60.0 4.4 %copy-start.40 = (f32[8,256]{1,0:T(8,128)S(1)}, f32[8,256]{1,0:T(8,128)}, u32[]{:S(2)}) copy-start(f32[8,256]{1,0:T(8,128)} %get-tuple-element.176) | copy-start | bytes 24580
  64.4 3.7 %copy-start.27 = (f32[8,256]{1,0:T(8,128)}, f32[8,256]{1,0:T(8,128)S(1)}, u32[]{:S(2)}) copy-start(f32[8,256]{1,0:T(8,128)S(1)} %get-tuple-element.145) | copy-start | bytes 24580
  73.0 25.8 %collective-permute-start = (f32[256,512]{1,0:T(8,128)}, f32[256,512]{1,0:T(8,128)S(1)}, u32[]{:S(2)}, u32[]{:S(2)}) collective-permute-start(f32[256,512]{1,0:T(8,128)} %copy.104), channel_id=1, source_target_pairs={{8,0},{16,8},{24,16},{9,1},{17,9},{25,17},{10,2},{18,10},{26,18},{... | collective-permute-start | bytes 1572872 | tf_op jit(solution)/shard_map/ppermute | solution.py:19
  74.7 12.8 %copy-start.21 = (f32[8,256]{1,0:T(8,128)S(1)}, f32[8,256]{1,0:T(8,128)}, u32[]{:S(2)}) copy-start(f32[8,256]{1,0:T(8,128)} %copy-done.20) | copy-start | bytes 24580
  74.7 12.8 %copy-start.23 = (f32[8,256]{1,0:T(8,128)S(1)}, f32[8,256]{1,0:T(8,128)}, u32[]{:S(2)}) copy-start(f32[8,256]{1,0:T(8,128)} %copy-done.22) | copy-start | bytes 24580
  74.7 12.8 %copy-start.32 = (f32[8,256]{1,0:T(8,128)S(1)}, f32[8,256]{1,0:T(8,128)}, u32[]{:S(2)}) copy-start(f32[8,256]{1,0:T(8,128)} %copy-done.31) | copy-start | bytes 24580
  74.7 13.4 %copy-start.3 = (f32[512,256,8]{1,0,2:T(8,128)S(1)}, f32[512,256,8]{1,0,2:T(8,128)}, u32[]{:S(2)}) copy-start(f32[512,256,8]{1,0,2:T(8,128)} %fusion.104) | copy-start | bytes 12582916
  74.7 13.4 %copy-start.41 = (f32[8,256]{1,0:T(8,128)S(1)}, f32[8,256]{1,0:T(8,128)}, u32[]{:S(2)}) copy-start(f32[8,256]{1,0:T(8,128)} %get-tuple-element.176) | copy-start | bytes 24580
  79.1 19.9 %collective-permute-start.1 = (bf16[256,1024]{1,0:T(8,128)(2,1)}, bf16[256,1024]{1,0:T(8,128)(2,1)S(1)}, u32[]{:S(2)}, u32[]{:S(2)}) collective-permute-start(bf16[256,1024]{1,0:T(8,128)(2,1)} %get-tuple-element.107), channel_id=1, source_target_pairs={{0,8},{8,0},{16,24},{24,16},{4,12},{12,4},{20,28},{28,20},{1,9},{9... | collective-permute-start | bytes 1572872 | tf_op jit(solution)/shard_map/ppermute | solution.py:126
  83.1 18.8 %collective-permute-start.2 = (bf16[256,1024]{1,0:T(8,128)(2,1)}, bf16[256,1024]{1,0:T(8,128)(2,1)S(1)}, u32[]{:S(2)}, u32[]{:S(2)}) collective-permute-start(bf16[256,1024]{1,0:T(8,128)(2,1)} %get-tuple-element.109), channel_id=1, source_target_pairs={{0,16},{8,24},{16,0},{24,8},{4,20},{12,28},{20,4},{28,12},{1,17},{... | collective-permute-start | bytes 1572872 | tf_op jit(solution)/shard_map/ppermute | solution.py:126
  86.0 23.7 %collective-permute-start.3 = (bf16[256,1024]{1,0:T(8,128)(2,1)}, bf16[256,1024]{1,0:T(8,128)(2,1)}, u32[]{:S(2)}, u32[]{:S(2)}) collective-permute-start(bf16[256,1024]{1,0:T(8,128)(2,1)} %get-tuple-element.121), channel_id=1, source_target_pairs={{0,24},{8,16},{16,8},{24,0},{4,28},{12,20},{20,12},{28,4},{1,25},{... | collective-permute-start | bytes 1572872 | tf_op jit(solution)/shard_map/ppermute | solution.py:126
  86.0 23.7 %collective-permute-start.4 = (bf16[256,1024]{1,0:T(8,128)(2,1)}, bf16[256,1024]{1,0:T(8,128)(2,1)}, u32[]{:S(2)}, u32[]{:S(2)}) collective-permute-start(bf16[256,1024]{1,0:T(8,128)(2,1)} %get-tuple-element.123), channel_id=1, source_target_pairs={{0,4},{8,12},{16,20},{24,28},{4,0},{12,8},{20,16},{28,24},{1,5},{9... | collective-permute-start | bytes 1572872 | tf_op jit(solution)/shard_map/ppermute | solution.py:126
  96.0 6.7 %copy-start.26 = (f32[256,1,8]{0,2,1:T(8,128)S(1)}, f32[256,1,8]{0,2,1:T(8,128)}, u32[]{:S(2)}) copy-start(f32[256,1,8]{0,2,1:T(8,128)} %subtract_bitcast_fusion) | copy-start | bytes 24580
  98.9 3.0 %copy-start.11 = (f32[256,512]{1,0:T(8,128)}, f32[256,512]{1,0:T(8,128)S(1)}, u32[]{:S(2)}) copy-start(f32[256,512]{1,0:T(8,128)S(1)} %collective-permute-done) | copy-start | bytes 1572868
  98.9 14.5 %collective-permute-start.5 = (bf16[256,1024]{1,0:T(8,128)(2,1)}, bf16[256,1024]{1,0:T(8,128)(2,1)S(1)}, u32[]{:S(2)}, u32[]{:S(2)}) collective-permute-start(bf16[256,1024]{1,0:T(8,128)(2,1)} %get-tuple-element.125), channel_id=1, source_target_pairs={{0,12},{8,4},{16,28},{24,20},{4,8},{12,0},{20,24},{28,16},{1,13},{... | collective-permute-start | bytes 1572872 | tf_op jit(solution)/shard_map/ppermute | solution.py:126
  99.0 27.2 %collective-permute-start.6 = (bf16[256,1024]{1,0:T(8,128)(2,1)}, bf16[256,1024]{1,0:T(8,128)(2,1)}, u32[]{:S(2)}, u32[]{:S(2)}) collective-permute-start(bf16[256,1024]{1,0:T(8,128)(2,1)} %get-tuple-element.127), channel_id=1, source_target_pairs={{0,20},{8,28},{16,4},{24,12},{4,16},{12,24},{20,0},{28,8},{1,21},{... | collective-permute-start | bytes 1572872 | tf_op jit(solution)/shard_map/ppermute | solution.py:126
  101.9 34.3 %collective-permute-start.7 = (bf16[256,1024]{1,0:T(8,128)(2,1)}, bf16[256,1024]{1,0:T(8,128)(2,1)}, u32[]{:S(2)}, u32[]{:S(2)}) collective-permute-start(bf16[256,1024]{1,0:T(8,128)(2,1)} %get-tuple-element.129), channel_id=1, source_target_pairs={{0,28},{8,20},{16,12},{24,4},{4,24},{12,16},{20,8},{28,0},{1,29},{... | collective-permute-start | bytes 1572872 | tf_op jit(solution)/shard_map/ppermute | solution.py:126
  113.4 22.8 %copy-start.10 = (bf16[256,1024]{1,0:T(8,128)(2,1)}, bf16[256,1024]{1,0:T(8,128)(2,1)S(1)}, u32[]{:S(2)}) copy-start(bf16[256,1024]{1,0:T(8,128)(2,1)S(1)} %collective-permute-done.5.refs_6_) | copy-start | bytes 1572868
  (21 other events, 48.8 us)
where the time goes:
time: 225 us
  Pallas kernels  120 us (53%)
  waiting for transfers between devices  27.4 us (12%)
  matrix products  27.3 us (12%)
  local copies, waits for them, and re-layouts  23.1 us (10%)
  other arithmetic  13.1 us (6%)
  starting transfers between devices  12.9 us (6%)
    pallas_call x1, Pallas kernels, tail(): pl.pallas_call(functools.partial(tail_kernel, fsdp, chips, cores, depth,...  84.3 us
    pallas_call x1, Pallas kernels, project(): pl.pallas_call(functools.partial(project_kernel, fsdp, chips, cores, chun...  35.4 us
    ppermute x7, waiting for transfers between devices, shift_plane(): return lax.ppermute(value, ('seq', 'fsdp'), pairs)  27.4 us
    unnamed x92, local copies, waits for them, and re-layouts  12 us
    ppermute x7, starting transfers between devices, shift_plane(): return lax.ppermute(value, ('seq', 'fsdp'), pairs)  11.4 us
    dot_general x4, matrix products, one_block(): jnp.einsum('kgrw,wkd->rkgd', slope, key_block, preferred_element_type=jnp...  10.3 us
    dot_general x4, matrix products, one_block(): jnp.einsum('rkgd,wkd->kgrw', queries, key_block, preferred_element_type=j...  9.8 us
    dot_general x4, matrix products, one_block(): jnp.einsum('kgrw,rkgd->wkd', slope, queries, preferred_element_type=jnp.f...  7.2 us
  transfers between devices with their start and end apart: 8, of which 4 were waited for; matrix products, arithmetic and copies ran while one was open for 10% of the time, Pallas kernels for 0%

commit v1 on v0

--- a/solution.py
+++ b/solution.py
@@ -220,29 +220,29 @@
         for item in group:
             accumulate(*item)
 
-    def part_copy(dz):
+    halves = final.shape[0]
+    piece = share // halves
+
+    def part_copy(dz, h):
         return remote(
-            ("part", dz), parts.at[dz - 1], landed.at[dz - 1], {"dp": lax.rem(z + dz, depth)}
-        )
-
-    for dz in range(1, depth):
-        row = pl.multiple_of(lax.rem(z + dz, depth) * share, share)
-        parts[dz - 1] = acc[pl.ds(row, share), :].astype(jnp.bfloat16)
-        part_copy(dz).start()
-    total = acc[pl.ds(pl.multiple_of(z * share, share), share), :]
-    for dz in range(1, depth):
-        part_copy(dz).wait_recv()
-        total = total + landed[dz - 1].astype(jnp.float32)
-    final[...] = (total * norm).astype(jnp.bfloat16)
-
-    def rows(dy, dc, zz):
+            ("part", dz, h), parts.at[h, dz - 1], landed.at[h, dz - 1],
+            {"dp": lax.rem(z + dz, depth)},
+        )
+
+    for h in range(halves):
+        for dz in range(1, depth):
+            row = pl.multiple_of(lax.rem(z + dz, depth) * share + h * piece, piece)
+            parts[h, dz - 1] = acc[pl.ds(row, piece), :].astype(jnp.bfloat16)
+            part_copy(dz, h).start()
+
+    def rows(dy, dc, zz, h):
         chip = lax.rem(y - dy + chips, chips)
         core = c if dc == 0 else 1 - c
-        row = ((chip * cores + core) * depth + zz) * share
-        return out_ref.at[pl.ds(pl.multiple_of(row, share), share)]
+        row = ((chip * cores + core) * depth + zz) * share + h * piece
+        return out_ref.at[pl.ds(pl.multiple_of(row, piece), piece)]
 
     def event_depth(event):
-        way, step = event
+        way, step, _ = event
         return z if way == 0 else z - way * (step + 1)
 
     def event_live(event):
@@ -250,49 +250,63 @@
         return (where >= 0) & (where < depth)
 
     def block_of(event):
-        return final if event[0] == 0 else rows(0, 0, event_depth(event))
+        h = event[2]
+        return final.at[h] if event[0] == 0 else rows(0, 0, event_depth(event), h)
 
     def depth_copy(event):
-        way, step = event
+        way, step, h = event
         where = z - way * step
-        src = final if step == 0 else rows(0, 0, where)
-        return remote(("z", event), src, rows(0, 0, where), {"dp": z + way})
+        src = final.at[h] if step == 0 else rows(0, 0, where, h)
+        return remote(("z", event), src, rows(0, 0, where, h), {"dp": z + way})
 
     def depth_live(event):
-        way, step = event
+        way, step, _ = event
         where = z - way * step
         return (where >= 0) & (where < depth) & (z + way >= 0) & (z + way < depth)
 
     def row_copy(event, dy, dc):
-        where = event_depth(event)
+        where, h = event_depth(event), event[2]
         if dc:
             return remote(
-                ("c", event, dy), rows(dy, 0, where) if dy else block_of(event),
-                rows(dy, 0, where), seq_at(0, 1),
+                ("c", event, dy), rows(dy, 0, where, h) if dy else block_of(event),
+                rows(dy, 0, where, h), seq_at(0, 1),
             )
-        return remote(("y", event, dy), block_of(event), rows(0, 0, where), seq_at(dy, 0))
-
-    own = (0, 0)
-    events = [own] + [(way, step) for step in range(depth - 1) for way in (1, -1)]
-    own_copy = pltpu.make_async_copy(final, rows(0, 0, z), local)
-    own_copy.start()
+        return remote(("y", event, dy), block_of(event), rows(0, 0, where, h), seq_at(dy, 0))
+
+    events = [(0, 0, h) for h in range(halves)]
+    for step in range(depth - 1):
+        events += [(way, step, h) for h in range(halves) for way in (1, -1)]
+
+    def own_copy(h):
+        return pltpu.make_async_copy(final.at[h], rows(0, 0, z, h), local.at[h])
 
     def when(event, live, action):
-        if event == own:
+        if event[0] == 0:
             action()
         else:
             pl.when(live(event))(action)
 
-    def spread(event):
+    def finish_sum(h):
+        total = acc[pl.ds(pl.multiple_of(z * share + h * piece, piece), piece), :]
+        for dz in range(1, depth):
+            part_copy(dz, h).wait_recv()
+            total = total + landed[h, dz - 1].astype(jnp.float32)
+        final[h] = (total * norm).astype(jnp.bfloat16)
+        own_copy(h).start()
+        if depth > 1:
+            for way in (1, -1):
+                first = (way, 0, h)
+                when(first, depth_live, lambda first=first: depth_copy(first).start())
+
+    def arrive(event):
+        if event[0] == 0:
+            finish_sum(event[2])
+        else:
+            depth_copy(event).wait_recv()
         for dy in range(1, chips):
             row_copy(event, dy, 0).start()
         if cores == 2:
             row_copy(event, 0, 1).start()
-
-    def arrive(event):
-        if event != own:
-            depth_copy(event).wait_recv()
-        spread(event)
 
     def relay(event):
         for dy in range(1, chips):
@@ -307,31 +321,33 @@
             for dy in range(chips):
                 row_copy(event, dy, 1).wait()
 
-    for way in (1, -1):
-        if depth > 1:
-            when((way, 0), depth_live, lambda way=way: depth_copy((way, 0)).start())
-    before = None
+    waiting = []
     for event in events:
         when(event, event_live, functools.partial(arrive, event))
-        if event != own and event[1] + 1 < depth - 1:
-            after_it = (event[0], event[1] + 1)
-            when(after_it, depth_live, lambda after_it=after_it: depth_copy(after_it).start())
-        if before is not None:
-            when(before, event_live, functools.partial(relay, before))
-        before = event
-    when(before, event_live, functools.partial(relay, before))
+        way, step, h = event
+        if way != 0 and step + 1 < depth - 1:
+            onward = (way, step + 1, h)
+            when(onward, depth_live, lambda onward=onward: depth_copy(onward).start())
+        waiting.append(event)
+        if len(waiting) > 2:
+            when(waiting[0], event_live, functools.partial(relay, waiting[0]))
+            waiting.pop(0)
+    for event in waiting:
+        when(event, event_live, functools.partial(relay, event))
     for event in events:
         when(event, event_live, functools.partial(close, event))
-        if event != own:
+        if event[0] != 0:
             when(event, depth_live, lambda event=event: depth_copy(event).wait_send())
-    own_copy.wait()
+        else:
+            own_copy(event[2]).wait()
     for df in range(fsdp):
         for dy in range(chips):
             for dc in range(cores):
                 if (df, dy, dc) != (0, 0, 0):
                     plane_copy(df, dy, dc).wait_send()
-    for dz in range(1, depth):
-        part_copy(dz).wait_send()
+    for h in range(halves):
+        for dz in range(1, depth):
+            part_copy(dz, h).wait_send()
 
 
 def tail(key_grad, token_blocks, norm):
@@ -342,7 +358,10 @@
     rows, slab = token_blocks[0].shape
     width = key_grad.shape[1]
     share = slab // depth
-    copies = count - 1 + depth - 1 + 2 * (depth - 1) + (2 * depth - 1) * (chips - 1 + chips)
+    halves = 2 if share % 32 == 0 else 1
+    copies = depth - 1 + 2 * (depth - 1) + (2 * depth - 1) * (chips - 1 + chips)
+    copies = count - 1 + halves * copies
+    pieces = pltpu.VMEM((halves, max(depth - 1, 1), share // halves, width), jnp.bfloat16)
     return pl.pallas_call(
         functools.partial(tail_kernel, fsdp, chips, cores, depth, share, norm),
         out_shape=jax.ShapeDtypeStruct((slab * parts, width), jnp.bfloat16),
@@ -351,12 +370,12 @@
         scratch_shapes=[
             pltpu.VMEM((count, rows, width), jnp.bfloat16),
             pltpu.VMEM((slab, width), jnp.float32),
-            pltpu.VMEM((max(depth - 1, 1), share, width), jnp.bfloat16),
-            pltpu.VMEM((max(depth - 1, 1), share, width), jnp.bfloat16),
-            pltpu.VMEM((share, width), jnp.bfloat16),
+            pieces,
+            pieces,
+            pltpu.VMEM((halves, share // halves, width), jnp.bfloat16),
             pltpu.SemaphoreType.DMA((copies,)),
             pltpu.SemaphoreType.DMA((copies,)),
-            pltpu.SemaphoreType.DMA(()),
+            pltpu.SemaphoreType.DMA((halves,)),
         ],
         compiler_params=pltpu.CompilerParams(collective_id=0, has_side_effects=True),
         name="tail",

time: 225 us -> 218 us (0.969)
  Pallas kernels: 120 us -> 112 us
    pallas_call x1, Pallas kernels: 84.3 us -> 77 us  [tail(): pl.pallas_call(functools.partial(tail_kernel, fsdp, chips, cores, depth,...]
where the time goes in v1:
time: 218 us
  Pallas kernels  112 us (51%)
  waiting for transfers between devices  27.4 us (13%)
  matrix products  27.3 us (13%)
  local copies, waits for them, and re-layouts  23.1 us (11%)
  other arithmetic  13.1 us (6%)
  starting transfers between devices  12.9 us (6%)
    pallas_call x1, Pallas kernels, tail(): pl.pallas_call(functools.partial(tail_kernel, fsdp, chips, cores, depth,...  77 us
    pallas_call x1, Pallas kernels, project(): pl.pallas_call(functools.partial(project_kernel, fsdp, chips, cores, chun...  35.4 us
    ppermute x7, waiting for transfers between devices, shift_plane(): return lax.ppermute(value, ('seq', 'fsdp'), pairs)  27.4 us
    unnamed x92, local copies, waits for them, and re-layouts  12 us
    ppermute x7, starting transfers between devices, shift_plane(): return lax.ppermute(value, ('seq', 'fsdp'), pairs)  11.4 us
    dot_general x4, matrix products, one_block(): jnp.einsum('kgrw,wkd->rkgd', slope, key_block, preferred_element_type=jnp...  10.3 us
    dot_general x4, matrix products, one_block(): jnp.einsum('rkgd,wkd->kgrw', queries, key_block, preferred_element_type=j...  9.8 us
    dot_general x4, matrix products, one_block(): jnp.einsum('kgrw,rkgd->wkd', slope, queries, preferred_element_type=jnp.f...  7.2 us
  transfers between devices with their start and end apart: 8, of which 4 were waited for; matrix products, arithmetic and copies ran while one was open for 10% of the time, Pallas kernels for 0%

profile of v1, /device:TPU:0, one launch (start us, length us, event | category | flops | bytes accessed | tf_op | source)
XLA Modules:
  0.0 217.7 jit_solution(1078513409185687370)
XLA Ops:
  0.6 3.3 %copy.60 = bf16[1,256,4096]{1,2,0:T(8,128)(2,1)S(1)} copy(bf16[1,256,4096]{2,1,0:T(8,128)(2,1)} %param.5) | data formatting | bytes 4194304 | tf_op args[0]
  3.9 35.4 %project.1 = bf16[512,512]{1,0:T(8,128)(2,1)} custom-call(bf16[256,8192]{1,0:T(8,128)(2,1)} %bitcast.324, bf16[4096,512]{1,0:T(8,128)(2,1)} %weight_hbm.1), custom_call_target="tpu_custom_call" | custom-call | tf_op jit(solution)/shard_map/project/pallas_call | solution.py:551
  39.3 1.2 reshape.347
  40.5 1.4 fusion.106
  42.2 2.7 %fusion.104 = f32[512,256,8]{1,0,2:T(8,128)} fusion(bf16[256,4,8,128]{0,3,2,1:T(8,128)(2,1)S(1)} %bitcast.326, bf16[512,1,128]{2,1,0:T(2,128)(2,1)S(1)} %get-tuple-element.174), kind=kOutput, calls=%fused_computation.88 | convolution fusion | flops 268435456 | bytes 4980736 | tf_op jit(solution)/shard_map/while/body/eval_jaxpr/rkgd,wkd->kgrw/dot_general | solution.py:53
  44.9 2.7 %fusion.103 = f32[512,256,8]{1,0,2:T(8,128)} fusion(bf16[256,4,8,128]{0,3,2,1:T(8,128)(2,1)S(1)} %bitcast.327, bf16[512,1,128]{2,1,0:T(2,128)(2,1)S(1)} %get-tuple-element.171), kind=kOutput, calls=%fused_computation.87 | convolution fusion | flops 268435456 | bytes 4980736 | tf_op jit(solution)/shard_map/while/body/eval_jaxpr/rkgd,wkd->kgrw/dot_general | solution.py:53
  50.2 1.4 copy-done
  51.6 1.8 copy-done.2
  53.5 3.6 %select_reduce_fusion.3 = (f32[8,256]{1,0:T(8,128)S(1)}, f32[8,256]{1,0:T(8,128)S(1)}, f32[8,256]{1,0:T(8,128)S(1)}, f32[8,256]{1,0:T(8,128)S(1)}, f32[512,256,8]{1,0,2:T(8,128)S(1)}) fusion(f32[512,256,8]{1,0,2:T(8,128)S(1)} %get-tuple-element.182, f32[8,256]{1,0:T(8,128)S(1)} %fusion.1, f32[8,256]{1,0:T(8,128)S(1)} %get-tuple-element.181, ...), kind=kOutput, calls=%fused_computation.14 | convolution fusion | flops 285204480 | bytes 17743872 | tf_op jit(solution)/shard_map/while/body/eval_jaxpr/rkgd,wkd->kgrw/dot_general | solution.py:53
  57.1 2.9 %fusion.3 = (f32[8,256]{1,0:T(8,128)S(1)}, f32[8,256]{1,0:T(8,128)S(1)}, f32[8,256]{1,0:T(8,128)S(1)}) fusion(f32[512,256,8]{1,0,2:T(8,128)S(1)} %get-tuple-element.183, f32[8,256]{1,0:T(8,128)S(1)} %get-tuple-element.142, pred[256,512]{0,1:T(8,128)(4,1)S(1)} %fusion.100, f32[8,256]{1,0:T(8,128)S(1)} %get-tuple-element.143, f32[512,256,8]{1,0,2:T(8,128)S(1)} %copy-done, ...), kind=kLoop, calls=%fused_computation.19 | loop fusion | flops 12576768 | bytes 12763136 | tf_op jit(solution)/shard_map/while/body/eval_jaxpr/reduce_sum | solution.py:59
  60.0 4.3 %select_reduce_fusion.2 = (f32[8,256]{1,0:T(8,128)S(1)}, f32[8,256]{1,0:T(8,128)S(1)}, f32[8,256]{1,0:T(8,128)S(1)}) fusion(f32[512,256,8]{1,0,2:T(8,128)S(1)} %get-tuple-element.183, f32[8,256]{1,0:T(8,128)S(1)} %get-tuple-element.148, f32[8,256]{1,0:T(8,128)S(1)} %get-tuple-element.142, pred[256,512]{0,1:T(8,128)(4,1)S(1)} %fusion.100, ...), kind=kLoop, calls=%fused_computation.11 | loop fusion | flops 22013952 | bytes 12787712 | tf_op jit(solution)/shard_map/while/body/eval_jaxpr/reduce_sum | solution.py:61
  64.5 1.8 fusion.79
  66.3 1.8 fusion.85
  68.2 1.8 fusion.91
  70.0 1.8 fusion.97
  73.0 1.5 collective-permute-start
  74.7 4.4 %dynamic-slice_bitcast_fusion = (bf16[256,1024]{1,0:T(8,128)(2,1)}, bf16[256,1024]{1,0:T(8,128)(2,1)}, bf16[256,1024]{1,0:T(8,128)(2,1)}, bf16[256,1024]{1,0:T(8...) fusion(bf16[1,256,8192]{2,1,0:T(8,128)(2,1)} %param.6, ...), kind=kLoop, calls=%fused_computation.74 | loop fusion | bytes 8388640 | tf_op jit(solution)/shard_map/dynamic_slice | solution.py:592
  79.1 4.0 %collective-permute-start.1 = (bf16[256,1024]{1,0:T(8,128)(2,1)}, bf16[256,1024]{1,0:T(8,128)(2,1)S(1)}, u32[]{:S(2)}, u32[]{:S(2)}) collective-permute-start(bf16[256,1024]{1,0:T(8,128)(2,1)} %get-tuple-element.107), channel_id=1, source_target_pairs={{0,8},{8,0},{16,24},{24,16},{4,12},{12,4},{20,28},{28,20},{1,9},{9... | collective-permute-start | bytes 1572872 | tf_op jit(solution)/shard_map/ppermute | solution.py:126
  83.1 2.9 %collective-permute-start.2 = (bf16[256,1024]{1,0:T(8,128)(2,1)}, bf16[256,1024]{1,0:T(8,128)(2,1)S(1)}, u32[]{:S(2)}, u32[]{:S(2)}) collective-permute-start(bf16[256,1024]{1,0:T(8,128)(2,1)} %get-tuple-element.109), channel_id=1, source_target_pairs={{0,16},{8,24},{16,0},{24,8},{4,20},{12,28},{20,4},{28,12},{1,17},{... | collective-permute-start | bytes 1572872 | tf_op jit(solution)/shard_map/ppermute | solution.py:126
  86.0 1.5 collective-permute-start.4
  88.2 2.6 %fusion.61 = bf16[256,1,8,128]{0,3,2,1:T(8,128)(2,1)} fusion(bf16[512,1,128]{2,1,0:T(2,128)(2,1)S(1)} %get-tuple-element.174, f32[512,256,8]{1,0,2:T(8,128)S(1)} %copy-done.3, f32[8,256]{1,0:T(8,128)S(1)} %copy-done.32, f32[8,256]{1,0:T(8,128)S(1)} %copy-done.23, f32[8,256]{1,0:T(8,128)S(1)} %copy-done.21, f32[8,256]{1,0:T(8,128)S(1)} %copy-done.41, ...), kind=kOutput, calls=%fused_computation.56 | convolution fusion | flops 278396928 | bytes 5013504 | tf_op jit(solution)/shard_map/while/body/eval_jaxpr/kgrw,wkd->rkgd/dot_general | solution.py:68
  90.8 2.6 %fusion.58 = bf16[256,1,8,128]{0,3,2,1:T(8,128)(2,1)} fusion(bf16[512,1,128]{2,1,0:T(2,128)(2,1)S(1)} %get-tuple-element.171, f32[512,256,8]{1,0,2:T(8,128)S(1)} %copy-done.1, f32[8,256]{1,0:T(8,128)S(1)} %copy-done.30, f32[8,256]{1,0:T(8,128)S(1)} %copy-done.19, f32[8,256]{1,0:T(8,128)S(1)} %copy-done.17, f32[8,256]{1,0:T(8,128)S(1)} %copy-done.39, ...), kind=kOutput, calls=%fused_computation.55 | convolution fusion | flops 278396928 | bytes 5013504 | tf_op jit(solution)/shard_map/while/body/eval_jaxpr/kgrw,wkd->rkgd/dot_general | solution.py:68
  93.4 2.6 %fusion.55 = bf16[256,1,8,128]{0,3,2,1:T(8,128)(2,1)} fusion(bf16[512,1,128]{2,1,0:T(2,128)(2,1)S(1)} %copy-done.13, f32[512,256,8]{1,0,2:T(8,128)S(1)} %copy-done.7, f32[8,256]{1,0:T(8,128)S(1)} %copy-done.28, f32[8,256]{1,0:T(8,128)S(1)} %copy-done.15, f32[8,256]{1,0:T(8,128)S(1)} %get-tuple-element.142, f32[8,256]{1,0:T(8,128)S(1)} %copy-done.37, ...), kind=kOutput, calls=%fused_computation.54 | convolution fusion | flops 278396928 | bytes 5013504 | tf_op jit(solution)/shard_map/while/body/eval_jaxpr/kgrw,wkd->rkgd/dot_general | solution.py:68
  96.0 2.6 %fusion.52 = bf16[256,1,8,128]{0,3,2,1:T(8,128)(2,1)} fusion(bf16[512,1,128]{2,1,0:T(2,128)(2,1)S(1)} %get-tuple-element.173, f32[512,256,8]{1,0,2:T(8,128)S(1)} %copy-done.5, f32[8,256]{1,0:T(8,128)S(1)} %copy-done.43, f32[8,256]{1,0:T(8,128)S(1)} %copy-done.25, f32[8,256]{1,0:T(8,128)S(1)} %get-tuple-element.181, f32[8,256]{1,0:T(8,128)S(1)} %copy-done.35, ...), kind=kOutput, calls=%fused_computation.53 | convolution fusion | flops 278396928 | bytes 5013504 | tf_op jit(solution)/shard_map/while/body/eval_jaxpr/kgrw,wkd->rkgd/dot_general | solution.py:68
  99.0 2.9 %collective-permute-start.6 = (bf16[256,1024]{1,0:T(8,128)(2,1)}, bf16[256,1024]{1,0:T(8,128)(2,1)}, u32[]{:S(2)}, u32[]{:S(2)}) collective-permute-start(bf16[256,1024]{1,0:T(8,128)(2,1)} %get-tuple-element.127), channel_id=1, source_target_pairs={{0,20},{8,28},{16,4},{24,12},{4,16},{12,24},{20,0},{28,8},{1,21},{... | collective-permute-start | bytes 1572872 | tf_op jit(solution)/shard_map/ppermute | solution.py:126
  103.3 1.8 pad_maximum_fusion
  106.0 2.8 %copy.86 = bf16[256,4096]{1,0:T(8,128)(2,1)} copy(bf16[256,4096]{0,1:T(8,128)(2,1)S(1)} %bitcast.325) | data formatting | bytes 4194304 | tf_op jit(solution)/shard_map/optimization_barrier | solution.py:635
  109.7 3.6 %collective-permute-done.5.refs_6_ = bf16[256,1024]{1,0:T(8,128)(2,1)S(1)} collective-permute-done((bf16[256,1024]{1,0:T(8,128)(2,1)}, bf16[256,1024]{1,0:T(8,128)(2,1)S(1)}, u32[]{:S(2)}, u32[]{:S(2)}) %collective-permute-start.5) | collective-permute-done | bytes 524320 | tf_op jit(solution)/shard_map/ppermute | solution.py:126
  113.4 12.8 %collective-permute-done.6.refs_7_ = bf16[256,1024]{1,0:T(8,128)(2,1)} collective-permute-done((bf16[256,1024]{1,0:T(8,128)(2,1)}, bf16[256,1024]{1,0:T(8,128)(2,1)}, u32[]{:S(2)}, u32[]{:S(2)}) %collective-permute-start.6) | collective-permute-done | bytes 524320 | tf_op jit(solution)/shard_map/ppermute | solution.py:126
  126.2 10.0 %collective-permute-done.7.refs_8_ = bf16[256,1024]{1,0:T(8,128)(2,1)} collective-permute-done((bf16[256,1024]{1,0:T(8,128)(2,1)}, bf16[256,1024]{1,0:T(8,128)(2,1)}, u32[]{:S(2)}, u32[]{:S(2)}) %collective-permute-start.7) | collective-permute-done | bytes 524320 | tf_op jit(solution)/shard_map/ppermute | solution.py:126
  136.2 77.0 %tail.1 = bf16[4096,512]{1,0:T(8,128)(2,1)} custom-call(bf16[256,512]{1,0:T(8,128)(2,1)} %add_convert_fusion.refs_0_, bf16[256,1024]{1,0:T(8,128)(2,1)} %get-tuple-element.106.refs_1_, bf16[256,1024]{1,0:T(8,128)(2,1)} %copy-done.8, bf16[256,1024]{1,0:T(8,128)(2,1)} %copy-done.9, bf16[256,1024]{1,0:T(8,128)(2,1)} %collective-permute-done.3.refs_4_, ...), custom_call_target="tpu_custom_call" | custom-call | tf_op jit(solution)/shard_map/tail/pallas_call | solution.py:365
  213.2 4.5 %copy.134 = bf16[4096,512]{1,0:T(8,128)(2,1)} copy(bf16[4096,512]{1,0:T(8,128)(2,1)} %tail.1) | data formatting | bytes 8388608
  (114 shorter events, 8.2 us)
Async XLA Ops:
  3.9 38.0 %copy-start.44 = (s32[1,8]{1,0:T(1,128)S(1)}, s32[1,8]{1,0:T(1,128)}, u32[]{:S(2)}) copy-start(s32[1,8]{1,0:T(1,128)} %param.8) | copy-start | bytes 100
  42.2 5.4 %copy-start.33 = (bf16[1,256,32]{1,2,0:T(8,128)(2,1)S(1)}, bf16[1,256,32]{1,2,0:T(8,128)(2,1)}, u32[]{:S(2)}) copy-start(bf16[1,256,32]{1,2,0:T(8,128)(2,1)} %param.9) | copy-start | bytes 49156
  48.5 3.2 %copy-start = (f32[512,256,8]{1,0,2:T(8,128)S(1)}, f32[512,256,8]{1,0,2:T(8,128)}, u32[]{:S(2)}) copy-start(f32[512,256,8]{1,0,2:T(8,128)} %fusion.103) | copy-start | bytes 12582916
  48.5 5.0 %copy-start.2 = (f32[512,256,8]{1,0,2:T(8,128)S(1)}, f32[512,256,8]{1,0,2:T(8,128)}, u32[]{:S(2)}) copy-start(f32[512,256,8]{1,0,2:T(8,128)} %fusion.104) | copy-start | bytes 12582916
  48.5 5.0 %copy-start.13 = (bf16[512,1,128]{2,1,0:T(2,128)(2,1)S(1)}, bf16[512,1,128]{2,1,0:T(2,128)(2,1)}, u32[]{:S(2)}) copy-start(bf16[512,1,128]{2,1,0:T(2,128)(2,1)} %get-tuple-element.172) | copy-start | bytes 393220
  49.3 20.7 %copy-start.4 = (f32[512,256,8]{1,0,2:T(8,128)}, f32[512,256,8]{1,0,2:T(8,128)S(1)}, u32[]{:S(2)}) copy-start(f32[512,256,8]{1,0,2:T(8,128)S(1)} %get-tuple-element.182) | copy-start | bytes 12582916
  50.2 19.8 %copy-start.24 = (f32[8,256]{1,0:T(8,128)}, f32[8,256]{1,0:T(8,128)S(1)}, u32[]{:S(2)}) copy-start(f32[8,256]{1,0:T(8,128)S(1)} %fusion.1) | copy-start | bytes 24580
  57.1 7.3 %copy-start.20 = (f32[8,256]{1,0:T(8,128)}, f32[8,256]{1,0:T(8,128)S(1)}, u32[]{:S(2)}) copy-start(f32[8,256]{1,0:T(8,128)S(1)} %get-tuple-element.144) | copy-start | bytes 24580
  57.1 9.2 %copy-start.16 = (f32[8,256]{1,0:T(8,128)}, f32[8,256]{1,0:T(8,128)S(1)}, u32[]{:S(2)}) copy-start(f32[8,256]{1,0:T(8,128)S(1)} %get-tuple-element.143) | copy-start | bytes 24580
  57.1 11.0 %copy-start.6 = (f32[512,256,8]{1,0,2:T(8,128)}, f32[512,256,8]{1,0,2:T(8,128)S(1)}, u32[]{:S(2)}) copy-start(f32[512,256,8]{1,0,2:T(8,128)S(1)} %get-tuple-element.183) | copy-start | bytes 12582916
  57.1 12.9 %copy-start.42 = (f32[8,256]{1,0:T(8,128)}, f32[8,256]{1,0:T(8,128)S(1)}, u32[]{:S(2)}) copy-start(f32[8,256]{1,0:T(8,128)S(1)} %get-tuple-element.141) | copy-start | bytes 24580
  60.0 4.4 %copy-start.22 = (f32[8,256]{1,0:T(8,128)}, f32[8,256]{1,0:T(8,128)S(1)}, u32[]{:S(2)}) copy-start(f32[8,256]{1,0:T(8,128)S(1)} %get-tuple-element.160) | copy-start | bytes 24580
  60.0 6.3 %copy-start.18 = (f32[8,256]{1,0:T(8,128)}, f32[8,256]{1,0:T(8,128)S(1)}, u32[]{:S(2)}) copy-start(f32[8,256]{1,0:T(8,128)S(1)} %get-tuple-element.149) | copy-start | bytes 24580
  60.0 8.1 %copy-start.14 = (f32[8,256]{1,0:T(8,128)}, f32[8,256]{1,0:T(8,128)S(1)}, u32[]{:S(2)}) copy-start(f32[8,256]{1,0:T(8,128)S(1)} %get-tuple-element.148) | copy-start | bytes 24580
  60.0 4.4 %copy-start.40 = (f32[8,256]{1,0:T(8,128)S(1)}, f32[8,256]{1,0:T(8,128)}, u32[]{:S(2)}) copy-start(f32[8,256]{1,0:T(8,128)} %get-tuple-element.176) | copy-start | bytes 24580
  64.4 3.7 %copy-start.27 = (f32[8,256]{1,0:T(8,128)}, f32[8,256]{1,0:T(8,128)S(1)}, u32[]{:S(2)}) copy-start(f32[8,256]{1,0:T(8,128)S(1)} %get-tuple-element.145) | copy-start | bytes 24580
  73.0 25.8 %collective-permute-start = (f32[256,512]{1,0:T(8,128)}, f32[256,512]{1,0:T(8,128)S(1)}, u32[]{:S(2)}, u32[]{:S(2)}) collective-permute-start(f32[256,512]{1,0:T(8,128)} %copy.104), channel_id=1, source_target_pairs={{8,0},{16,8},{24,16},{9,1},{17,9},{25,17},{10,2},{18,10},{26,18},{... | collective-permute-start | bytes 1572872 | tf_op jit(solution)/shard_map/ppermute | solution.py:19
  74.7 12.8 %copy-start.21 = (f32[8,256]{1,0:T(8,128)S(1)}, f32[8,256]{1,0:T(8,128)}, u32[]{:S(2)}) copy-start(f32[8,256]{1,0:T(8,128)} %copy-done.20) | copy-start | bytes 24580
  74.7 12.8 %copy-start.23 = (f32[8,256]{1,0:T(8,128)S(1)}, f32[8,256]{1,0:T(8,128)}, u32[]{:S(2)}) copy-start(f32[8,256]{1,0:T(8,128)} %copy-done.22) | copy-start | bytes 24580
  74.7 12.8 %copy-start.32 = (f32[8,256]{1,0:T(8,128)S(1)}, f32[8,256]{1,0:T(8,128)}, u32[]{:S(2)}) copy-start(f32[8,256]{1,0:T(8,128)} %copy-done.31) | copy-start | bytes 24580
  74.7 13.4 %copy-start.3 = (f32[512,256,8]{1,0,2:T(8,128)S(1)}, f32[512,256,8]{1,0,2:T(8,128)}, u32[]{:S(2)}) copy-start(f32[512,256,8]{1,0,2:T(8,128)} %fusion.104) | copy-start | bytes 12582916
  74.7 13.4 %copy-start.41 = (f32[8,256]{1,0:T(8,128)S(1)}, f32[8,256]{1,0:T(8,128)}, u32[]{:S(2)}) copy-start(f32[8,256]{1,0:T(8,128)} %get-tuple-element.176) | copy-start | bytes 24580
  79.1 19.9 %collective-permute-start.1 = (bf16[256,1024]{1,0:T(8,128)(2,1)}, bf16[256,1024]{1,0:T(8,128)(2,1)S(1)}, u32[]{:S(2)}, u32[]{:S(2)}) collective-permute-start(bf16[256,1024]{1,0:T(8,128)(2,1)} %get-tuple-element.107), channel_id=1, source_target_pairs={{0,8},{8,0},{16,24},{24,16},{4,12},{12,4},{20,28},{28,20},{1,9},{9... | collective-permute-start | bytes 1572872 | tf_op jit(solution)/shard_map/ppermute | solution.py:126
  83.1 18.8 %collective-permute-start.2 = (bf16[256,1024]{1,0:T(8,128)(2,1)}, bf16[256,1024]{1,0:T(8,128)(2,1)S(1)}, u32[]{:S(2)}, u32[]{:S(2)}) collective-permute-start(bf16[256,1024]{1,0:T(8,128)(2,1)} %get-tuple-element.109), channel_id=1, source_target_pairs={{0,16},{8,24},{16,0},{24,8},{4,20},{12,28},{20,4},{28,12},{1,17},{... | collective-permute-start | bytes 1572872 | tf_op jit(solution)/shard_map/ppermute | solution.py:126
  86.0 23.7 %collective-permute-start.3 = (bf16[256,1024]{1,0:T(8,128)(2,1)}, bf16[256,1024]{1,0:T(8,128)(2,1)}, u32[]{:S(2)}, u32[]{:S(2)}) collective-permute-start(bf16[256,1024]{1,0:T(8,128)(2,1)} %get-tuple-element.121), channel_id=1, source_target_pairs={{0,24},{8,16},{16,8},{24,0},{4,28},{12,20},{20,12},{28,4},{1,25},{... | collective-permute-start | bytes 1572872 | tf_op jit(solution)/shard_map/ppermute | solution.py:126
  86.0 23.7 %collective-permute-start.4 = (bf16[256,1024]{1,0:T(8,128)(2,1)}, bf16[256,1024]{1,0:T(8,128)(2,1)}, u32[]{:S(2)}, u32[]{:S(2)}) collective-permute-start(bf16[256,1024]{1,0:T(8,128)(2,1)} %get-tuple-element.123), channel_id=1, source_target_pairs={{0,4},{8,12},{16,20},{24,28},{4,0},{12,8},{20,16},{28,24},{1,5},{9... | collective-permute-start | bytes 1572872 | tf_op jit(solution)/shard_map/ppermute | solution.py:126
  96.0 6.7 %copy-start.26 = (f32[256,1,8]{0,2,1:T(8,128)S(1)}, f32[256,1,8]{0,2,1:T(8,128)}, u32[]{:S(2)}) copy-start(f32[256,1,8]{0,2,1:T(8,128)} %subtract_bitcast_fusion) | copy-start | bytes 24580
  98.9 3.0 %copy-start.11 = (f32[256,512]{1,0:T(8,128)}, f32[256,512]{1,0:T(8,128)S(1)}, u32[]{:S(2)}) copy-start(f32[256,512]{1,0:T(8,128)S(1)} %collective-permute-done) | copy-start | bytes 1572868
  98.9 14.5 %collective-permute-start.5 = (bf16[256,1024]{1,0:T(8,128)(2,1)}, bf16[256,1024]{1,0:T(8,128)(2,1)S(1)}, u32[]{:S(2)}, u32[]{:S(2)}) collective-permute-start(bf16[256,1024]{1,0:T(8,128)(2,1)} %get-tuple-element.125), channel_id=1, source_target_pairs={{0,12},{8,4},{16,28},{24,20},{4,8},{12,0},{20,24},{28,16},{1,13},{... | collective-permute-start | bytes 1572872 | tf_op jit(solution)/shard_map/ppermute | solution.py:126
  99.0 27.2 %collective-permute-start.6 = (bf16[256,1024]{1,0:T(8,128)(2,1)}, bf16[256,1024]{1,0:T(8,128)(2,1)}, u32[]{:S(2)}, u32[]{:S(2)}) collective-permute-start(bf16[256,1024]{1,0:T(8,128)(2,1)} %get-tuple-element.127), channel_id=1, source_target_pairs={{0,20},{8,28},{16,4},{24,12},{4,16},{12,24},{20,0},{28,8},{1,21},{... | collective-permute-start | bytes 1572872 | tf_op jit(solution)/shard_map/ppermute | solution.py:126
  101.9 34.3 %collective-permute-start.7 = (bf16[256,1024]{1,0:T(8,128)(2,1)}, bf16[256,1024]{1,0:T(8,128)(2,1)}, u32[]{:S(2)}, u32[]{:S(2)}) collective-permute-start(bf16[256,1024]{1,0:T(8,128)(2,1)} %get-tuple-element.129), channel_id=1, source_target_pairs={{0,28},{8,20},{16,12},{24,4},{4,24},{12,16},{20,8},{28,0},{1,29},{... | collective-permute-start | bytes 1572872 | tf_op jit(solution)/shard_map/ppermute | solution.py:126
  113.4 22.8 %copy-start.10 = (bf16[256,1024]{1,0:T(8,128)(2,1)}, bf16[256,1024]{1,0:T(8,128)(2,1)S(1)}, u32[]{:S(2)}) copy-start(bf16[256,1024]{1,0:T(8,128)(2,1)S(1)} %collective-permute-done.5.refs_6_) | copy-start | bytes 1572868
  (21 other events, 48.8 us)
